TPU v7x, 32 devices: a whole 2x2x4 slice. The times are simulated.
32 devices in a mesh: row: 8 (over z, y), col: 4 (over x, core).
Axes of the slice: x: 2, y: 2, z: 4, core: 2. Of those that a mesh axis runs over, the one named last changes fastest.
Arguments:
- queries: bfloat16 [12288, 4096], P(('row', 'col')), may hold values from -6 to 6
- keys: bfloat16 [16384, 256], P(('row', 'col')), may hold values from -6 to 6
- values: bfloat16 [16384, 256], P(('row', 'col')), may hold values from -6 to 6
- output_gradient: bfloat16 [12288, 4096], P(('row', 'col')), may hold values from -6 to 6
- tile_block_table: int32 [96, 3], P(('row', 'col')), may hold values from 0 to 31, as said below
Outputs:
- dqueries: bfloat16 [12288, 4096], P(('row', 'col'))
- dkeys: bfloat16 [16384, 256], P(('row', 'col'))
- dvalues: bfloat16 [16384, 256], P(('row', 'col'))
Inputs may be any that keep to these rules, and one draw needn't show every extreme that they name: `tile_block_table`: A tile's first id is the block that holds its own query rows; its 3 ids are distinct and none is larger than that block. Block b is held by the device of index b // 1 in the order row-major over (row, col). The tiles of one device name at most 1 distinct blocks held on devices of one col index, and at most 2 distinct blocks held on devices of one row index.
All inputs are finite; a program needn't handle non-finite values.
Results may differ from a plain program's by a relative error of at most 0.0064.
Values may be sent and summed in bfloat16 or wider, within the bound.
No kernel may reach another device: no remote copies, remote signals or barrier semaphores. Data moves between devices by JAX's collectives and lax.ppermute only.
A program may use at most 192 MiB of HBM per device.

v0:
```python
import jax
import jax.numpy as jnp
from jax import lax
from jax.sharding import PartitionSpec as P

QUERY_HEADS = 32
KEY_VALUE_HEADS = 2
HEAD_WIDTH = 128
GROUP_WIDTH = 16
TILE_QUERY_ROWS = 128
BLOCK_KEY_ROWS = 512
PICKED_BLOCKS = 3


def pair_grads(
    tile_query_rows, gradient_rows, block_key_rows, block_value_rows, query_place, key_place
):
    factor = HEAD_WIDTH ** (-0.5)
    forward = (((1,), (1,)), ((), ()))
    backward = (((0,), (0,)), ((), ()))
    scores = (
        lax.dot_general(
            tile_query_rows, block_key_rows, forward, preferred_element_type=jnp.float32
        )
        * factor
    )
    scores = jnp.where(key_place[None, :] <= query_place[:, None], scores, -jnp.inf)
    weights = jax.nn.softmax(scores, axis=-1)
    grad_weights = lax.dot_general(
        gradient_rows, block_value_rows, forward, preferred_element_type=jnp.float32
    )
    row_delta = jnp.sum(weights * grad_weights, axis=-1, keepdims=True)
    grad_scores = (weights * (grad_weights - row_delta) * factor).astype(jnp.bfloat16)
    query_gradient = jnp.dot(grad_scores, block_key_rows, preferred_element_type=jnp.float32)
    key_gradient = lax.dot_general(
        grad_scores, tile_query_rows, backward, preferred_element_type=jnp.float32
    )
    value_gradient = lax.dot_general(
        weights.astype(jnp.bfloat16), gradient_rows, backward, preferred_element_type=jnp.float32
    )
    return (query_gradient, key_gradient, value_gradient)


def item_grads(packed):
    query_item, gradient_item, block_item, query_place, key_place = packed
    return pair_grads(
        query_item, gradient_item, block_item[0], block_item[1], query_place, key_place
    )


def local(queries, keys, values, output_gradient, tile_block_table):
    n_row = lax.axis_size("row")
    n_col = lax.axis_size("col")
    my_row = lax.axis_index("row")
    my_col = lax.axis_index("col")
    devices = n_row * n_col
    my_device = my_row * n_col + my_col
    blk_dev = keys.shape[0] // BLOCK_KEY_ROWS
    device_tile_count = tile_block_table.shape[0]
    kv_width = keys.shape[1]
    cap_row = 2 * blk_dev
    nblocks = devices * blk_dev
    band_rows = n_row * blk_dev
    flat_width = BLOCK_KEY_ROWS * 2 * kv_width
    starting_position = nblocks * BLOCK_KEY_ROWS - devices * device_tile_count * TILE_QUERY_ROWS
    catalog = jnp.arange(nblocks, dtype=jnp.int32)
    row_lists = lax.all_gather(tile_block_table, "col", axis=0, tiled=True)
    wanted = jnp.any(
        row_lists.reshape(n_col, device_tile_count * PICKED_BLOCKS, 1) == catalog, axis=1
    ).astype(jnp.int32)
    layout = wanted.reshape(n_col, n_row, n_col, blk_dev)
    by_col = jnp.transpose(layout, (0, 2, 1, 3)).reshape(n_col, n_col, band_rows)
    col_rank = jnp.cumsum(by_col, axis=2) - by_col
    local_kv = jnp.concatenate((keys, values), axis=1)
    column = lax.all_gather(local_kv, "row", axis=0, tiled=True).reshape(band_rows, flat_width)
    row_wants = by_col[:, my_col, :]
    row_ranks = col_rank[:, my_col, :]
    slot_ids = jnp.arange(blk_dev, dtype=jnp.int32)
    picker = (row_ranks[:, None, :] == slot_ids[None, :, None]) & (row_wants[:, None, :] == 1)
    picker = picker.astype(jnp.bfloat16).reshape(n_col * blk_dev, band_rows)
    outgoing = jnp.dot(picker, column, preferred_element_type=jnp.float32).astype(jnp.bfloat16)
    landed_parts = lax.all_to_all(
        outgoing.reshape(n_col, blk_dev, flat_width), "col", split_axis=0, concat_axis=0, tiled=True
    )
    landed_parts = landed_parts.reshape(n_col * blk_dev, BLOCK_KEY_ROWS, 2 * kv_width)
    my_lists = tile_block_table.reshape(device_tile_count * PICKED_BLOCKS)
    holder = my_lists // blk_dev
    holder_row = holder // n_col
    holder_col = holder % n_col
    within = my_lists % blk_dev
    my_ranks = col_rank[my_col]
    paired_position = holder_col * blk_dev + my_ranks[holder_col, holder_row * blk_dev + within]
    paired_key_value = jnp.take(landed_parts, paired_position, axis=0).reshape(
        device_tile_count, PICKED_BLOCKS * BLOCK_KEY_ROWS, 2, KEY_VALUE_HEADS, HEAD_WIDTH
    )
    entry_count = device_tile_count * KEY_VALUE_HEADS
    tile_query_rows = queries.reshape(
        device_tile_count, TILE_QUERY_ROWS, KEY_VALUE_HEADS, GROUP_WIDTH, HEAD_WIDTH
    ).transpose(0, 2, 3, 1, 4)
    tile_query_rows = tile_query_rows.reshape(
        entry_count, GROUP_WIDTH * TILE_QUERY_ROWS, HEAD_WIDTH
    )
    gradient_rows = output_gradient.reshape(
        device_tile_count, TILE_QUERY_ROWS, KEY_VALUE_HEADS, GROUP_WIDTH, HEAD_WIDTH
    ).transpose(0, 2, 3, 1, 4)
    gradient_rows = gradient_rows.reshape(entry_count, GROUP_WIDTH * TILE_QUERY_ROWS, HEAD_WIDTH)
    block_rows = paired_key_value.transpose(0, 3, 2, 1, 4).reshape(
        entry_count, 2, PICKED_BLOCKS * BLOCK_KEY_ROWS, HEAD_WIDTH
    )
    global_tile_index = my_device * device_tile_count + jnp.arange(
        device_tile_count, dtype=jnp.int32
    )
    rows_per_head = jnp.arange(GROUP_WIDTH * TILE_QUERY_ROWS, dtype=jnp.int32) % TILE_QUERY_ROWS
    query_place = jnp.repeat(
        starting_position + global_tile_index[:, None] * TILE_QUERY_ROWS + rows_per_head[None, :],
        KEY_VALUE_HEADS,
        axis=0,
    )
    row_offsets = jnp.arange(BLOCK_KEY_ROWS, dtype=jnp.int32)
    key_place = jnp.repeat(
        (tile_block_table[:, :, None] * BLOCK_KEY_ROWS + row_offsets).reshape(
            device_tile_count, PICKED_BLOCKS * BLOCK_KEY_ROWS
        ),
        KEY_VALUE_HEADS,
        axis=0,
    )
    query_gradient, key_gradient, value_gradient = lax.map(
        item_grads, (tile_query_rows, gradient_rows, block_rows, query_place, key_place)
    )
    dqueries = query_gradient.reshape(
        device_tile_count, KEY_VALUE_HEADS, GROUP_WIDTH, TILE_QUERY_ROWS, HEAD_WIDTH
    ).transpose(0, 3, 1, 2, 4)
    dqueries = dqueries.reshape(
        device_tile_count * TILE_QUERY_ROWS, QUERY_HEADS * HEAD_WIDTH
    ).astype(jnp.bfloat16)
    paired_terms = jnp.stack((key_gradient, value_gradient), axis=0).reshape(
        2, device_tile_count, KEY_VALUE_HEADS, PICKED_BLOCKS, BLOCK_KEY_ROWS, HEAD_WIDTH
    )
    paired_terms = paired_terms.transpose(1, 3, 4, 0, 2, 5).reshape(
        device_tile_count * PICKED_BLOCKS, flat_width
    )
    row_span = n_col * blk_dev
    col_lists = lax.all_gather(tile_block_table, "row", axis=0, tiled=True)
    col_wanted = jnp.any(
        col_lists.reshape(n_row, device_tile_count * PICKED_BLOCKS, 1) == catalog, axis=1
    ).astype(jnp.int32)
    by_row = col_wanted.reshape(n_row, n_row, row_span)
    row_rank = jnp.cumsum(by_row, axis=2) - by_row
    own_ranks = row_rank[my_row]
    row_slot = holder_row * cap_row + own_ranks[holder_row, holder_col * blk_dev + within]
    slot_count = n_row * cap_row
    assign = (row_slot[None, :] == jnp.arange(slot_count, dtype=jnp.int32)[:, None]).astype(
        jnp.float32
    )
    partials = jnp.dot(
        assign, paired_terms, precision=lax.Precision.HIGHEST, preferred_element_type=jnp.float32
    ).astype(jnp.bfloat16)
    returned = lax.all_to_all(
        partials.reshape(n_row, cap_row, flat_width), "row", split_axis=0, concat_axis=0, tiled=True
    )
    returned = returned.reshape(slot_count, flat_width)
    sender_wants = by_row[:, my_row, :]
    sender_ranks = row_rank[:, my_row, :]
    row_slot_ids = jnp.arange(cap_row, dtype=jnp.int32)
    collect = (sender_ranks[:, None, :] == row_slot_ids[None, :, None]) & (
        sender_wants[:, None, :] == 1
    )
    collect = collect.astype(jnp.bfloat16).reshape(slot_count, row_span).T
    result = lax.psum_scatter(
        jnp.dot(collect, returned, preferred_element_type=jnp.float32),
        "col",
        scatter_dimension=0,
        tiled=True,
    )
    result = result.reshape(blk_dev * BLOCK_KEY_ROWS, 2 * kv_width)
    return (
        dqueries,
        result[:, :kv_width].astype(jnp.bfloat16),
        result[:, kv_width:].astype(jnp.bfloat16),
    )


def solution(mesh):
    return jax.shard_map(
        local,
        mesh=mesh,
        in_specs=(
            P(("row", "col"), None),
            P(("row", "col"), None),
            P(("row", "col"), None),
            P(("row", "col"), None),
            P(("row", "col"), None),
        ),
        out_specs=(P(("row", "col"), None), P(("row", "col"), None), P(("row", "col"), None)),
        check_vma=False,
    )
```

profile of v0, /device:TPU:0, one launch (start us, length us, event | category | flops | bytes accessed | tf_op | source)
XLA Modules:
  0.0 771.3 jit_solution(15225292182704396535)
XLA Ops:
  9.9 6.3 all-gather
  19.3 66.9 %all-gather.4.cloned.1.call-done = bf16[4096,512]{1,0:T(8,128)(2,1)} async-done(((bf16[512,512]{1,0:T(8,128)(2,1)}), bf16[4096,512]{1,0:T(8,128)(2,1)}) %all-gather.4.cloned.1.call-update) | async-done | bytes 4194320 | tf_op jit(solution)/shard_map/all_gather | solution.py:75
  86.2 6.0 reshape.352
  92.3 4.7 fusion.27
  119.2 26.1 %all-gather.1 = s32[8,3,3]{2,1,0:T(4,128)S(1)} all-gather(s32[1,3,3]{2,1,0:T(4,128)S(1)} %bitcast.153), channel_id=1, replica_groups=mesh['row'=8,'col'=4] {'row'}, dimensions={0}, use_global_device_ids=true | all-gather | bytes 324 | tf_op jit(solution)/shard_map/all_gather | solution.py:143
  150.6 14.8 %reduce.2 = bf16[4,262144]{1,0:T(4,128)(2,1)} reduce(bf16[4,1,262144]{2,1,0:T(2,128)(2,1)} %reshape.399, bf16[]{:T(256)} %constant.180), dimensions={1}, to_apply=%all_to_all.6.reduce_sub_computation | reduce | bytes 4194306 | tf_op jit(solution)/shard_map/all_to_all | solution.py:82
  171.0 7.8 %gather.20 = bf16[3,1536,2,2,128]{4,3,2,1,0:T(2,128)(2,1)} reshape(bf16[9,512,512]{2,1,0:T(8,128)(2,1)} %gather_fusion.1) | data formatting | bytes 9437184 | tf_op jit(solution)/shard_map/jit(_take)/gather | solution.py:93
  178.8 11.5 %fusion.29 = bf16[3,2,2,1536,128]{4,1,2,3,0:T(2,128)(2,1)S(1)} fusion(bf16[3,1536,2,2,128]{4,3,2,1,0:T(2,128)(2,1)} %gather.20, pred[3,1536]{1,0:T(4,128)(4,1)S(1)} %bitcast.154), kind=kLoop, calls=%fused_computation.42 | loop fusion | flops 2359296 | bytes 9441792 | tf_op jit(solution)/shard_map/transpose | solution.py:107
  193.2 226.3 %while.14 = (s32[]{:T(128)}, bf16[6,2048,128]{2,1,0:T(8,128)(2,1)S(1)}, f32[6,1536,128]{2,1,0:T(8,128)}, f32[6,1536,128]{2,1,0:T(8,128)}, s32[6,1536]{1,0:T(8,12...) while((s32[]{:T(128)}, ...), condition=%wide.region_6.7_spmd, body=%wide.region_2.6_spmd.sunk | while | flops 4086294528 | bytes 213654736 | solution.py:127
  205.8 12.0 %multiply_reduce_fusion.2 = (f32[2048]{0:T(1024)S(1)}, f32[2048,1536]{0,1:T(8,128)}) fusion(f32[2048]{0:T(1024)S(1)} %fusion.73, f32[2048,1536]{0,1:T(8,128)} %copy-done, f32[2048]{0:T(1024)S(1)} %get-tuple-element.142, bf16[6,2,1536,128]{3,2,1,0:T(8,128)(2,1)} %get-tuple-element.176, s32[]{:T(128)} %get-tuple-element.157, s32[]{:T(128)S(6)} %add.285, ...), kind=kOutput, calls=%fused_computation.4.clone.1 | convolution fusion | flops 817887232 | bytes 26108932 | tf_op jit(solution)/shard_map/while/body/eval_jaxpr/dot_general | solution.py:29
  217.8 6.7 multiply_convert_fusion.2
  243.5 12.0 %multiply_reduce_fusion.2 = (f32[2048]{0:T(1024)S(1)}, f32[2048,1536]{0,1:T(8,128)}) fusion(f32[2048]{0:T(1024)S(1)} %fusion.73, f32[2048,1536]{0,1:T(8,128)} %copy-done, f32[2048]{0:T(1024)S(1)} %get-tuple-element.142, bf16[6,2,1536,128]{3,2,1,0:T(8,128)(2,1)} %get-tuple-element.176, s32[]{:T(128)} %get-tuple-element.157, s32[]{:T(128)S(6)} %add.285, ...), kind=kOutput, calls=%fused_computation.4.clone.1 | convolution fusion | flops 817887232 | bytes 26108932 | tf_op jit(solution)/shard_map/while/body/eval_jaxpr/dot_general | solution.py:29
  255.5 6.7 multiply_convert_fusion.2
  281.1 12.0 %multiply_reduce_fusion.2 = (f32[2048]{0:T(1024)S(1)}, f32[2048,1536]{0,1:T(8,128)}) fusion(f32[2048]{0:T(1024)S(1)} %fusion.73, f32[2048,1536]{0,1:T(8,128)} %copy-done, f32[2048]{0:T(1024)S(1)} %get-tuple-element.142, bf16[6,2,1536,128]{3,2,1,0:T(8,128)(2,1)} %get-tuple-element.176, s32[]{:T(128)} %get-tuple-element.157, s32[]{:T(128)S(6)} %add.285, ...), kind=kOutput, calls=%fused_computation.4.clone.1 | convolution fusion | flops 817887232 | bytes 26108932 | tf_op jit(solution)/shard_map/while/body/eval_jaxpr/dot_general | solution.py:29
  293.1 6.7 multiply_convert_fusion.2
  318.7 12.0 %multiply_reduce_fusion.2 = (f32[2048]{0:T(1024)S(1)}, f32[2048,1536]{0,1:T(8,128)}) fusion(f32[2048]{0:T(1024)S(1)} %fusion.73, f32[2048,1536]{0,1:T(8,128)} %copy-done, f32[2048]{0:T(1024)S(1)} %get-tuple-element.142, bf16[6,2,1536,128]{3,2,1,0:T(8,128)(2,1)} %get-tuple-element.176, s32[]{:T(128)} %get-tuple-element.157, s32[]{:T(128)S(6)} %add.285, ...), kind=kOutput, calls=%fused_computation.4.clone.1 | convolution fusion | flops 817887232 | bytes 26108932 | tf_op jit(solution)/shard_map/while/body/eval_jaxpr/dot_general | solution.py:29
  330.7 6.7 multiply_convert_fusion.2
  356.3 12.0 %multiply_reduce_fusion.2 = (f32[2048]{0:T(1024)S(1)}, f32[2048,1536]{0,1:T(8,128)}) fusion(f32[2048]{0:T(1024)S(1)} %fusion.73, f32[2048,1536]{0,1:T(8,128)} %copy-done, f32[2048]{0:T(1024)S(1)} %get-tuple-element.142, bf16[6,2,1536,128]{3,2,1,0:T(8,128)(2,1)} %get-tuple-element.176, s32[]{:T(128)} %get-tuple-element.157, s32[]{:T(128)S(6)} %add.285, ...), kind=kOutput, calls=%fused_computation.4.clone.1 | convolution fusion | flops 817887232 | bytes 26108932 | tf_op jit(solution)/shard_map/while/body/eval_jaxpr/dot_general | solution.py:29
  368.3 6.7 multiply_convert_fusion.2
  393.9 12.0 %multiply_reduce_fusion.2 = (f32[2048]{0:T(1024)S(1)}, f32[2048,1536]{0,1:T(8,128)}) fusion(f32[2048]{0:T(1024)S(1)} %fusion.73, f32[2048,1536]{0,1:T(8,128)} %copy-done, f32[2048]{0:T(1024)S(1)} %get-tuple-element.142, bf16[6,2,1536,128]{3,2,1,0:T(8,128)(2,1)} %get-tuple-element.176, s32[]{:T(128)} %get-tuple-element.157, s32[]{:T(128)S(6)} %add.285, ...), kind=kOutput, calls=%fused_computation.4.clone.1 | convolution fusion | flops 817887232 | bytes 26108932 | tf_op jit(solution)/shard_map/while/body/eval_jaxpr/dot_general | solution.py:29
  405.9 6.7 multiply_convert_fusion.2
  419.6 7.1 copy.68
  426.7 6.0 copy.69
  432.7 5.5 maximum_bitcast_fusion
  438.2 22.1 %reshape.359 = f32[9,262144]{1,0:T(8,128)} reshape(f32[3,3,512,2,2,128]{5,4,3,2,1,0:T(2,128)} %maximum_bitcast_fusion) | data formatting | bytes 18874368 | tf_op jit(solution)/shard_map/reshape | solution.py:139
  460.3 13.9 %convolution_convert_fusion = bf16[16,262144]{1,0:T(8,128)(2,1)} fusion(f32[9,262144]{1,0:T(8,128)} %reshape.359, s32[9]{0:T(128)S(1)} %copy-done.8), kind=kOutput, calls=%fused_computation.35 | convolution fusion | flops 457179264 | bytes 17825828 | tf_op jit(solution)/shard_map/dot_general | solution.py:155
  474.2 9.7 %reshape.360 = bf16[8,2,262144]{2,1,0:T(2,128)(2,1)} reshape(bf16[16,262144]{1,0:T(8,128)(2,1)} %convolution_convert_fusion) | data formatting | bytes 16777216 | tf_op jit(solution)/shard_map/reshape | solution.py:159
  483.9 5.1 all-to-all-start.1
  498.2 170.2 %all-to-all-done.1 = bf16[8,2,262144]{2,1,0:T(2,128)(2,1)} async-done(((bf16[8,2,262144]{2,1,0:T(2,128)(2,1)}), bf16[8,2,262144]{2,1,0:T(2,128)(2,1)}, u32[]{:S(2)}, u32[]{:S(2)}) %all-to-all-start.1) | async-done | bytes 8388640 | tf_op jit(solution)/shard_map/all_to_all | solution.py:158
  668.4 10.5 %convolution_bitcast_fusion.2 = f32[4,262144]{1,0:T(4,128)} fusion(bf16[8,2,262144]{2,1,0:T(2,128)(2,1)} %all-to-all-done.1, s32[8,4]{0,1:T(4,128)S(1)} %dynamic-slice_bitcast_fusion.5, pred[8,4]{0,1:T(4,128)(4,1)S(1)} %fusion.43), kind=kOutput, calls=%fused_computation.36 | convolution fusion | flops 33554560 | bytes 12583072 | tf_op jit(solution)/shard_map/dot_general | solution.py:170
  678.9 76.0 %all-reduce.2 = bf16[4,262144]{1,0:T(4,128)(2,1)S(1)} all-reduce(f32[4,262144]{1,0:T(4,128)} %convolution_bitcast_fusion.2), channel_id=2, replica_groups=mesh['row'=8,'col'=4] {'col'}, use_global_device_ids=true, to_apply=%region_9.10.clone | all-reduce | flops 1048576 | bytes 6291456
  754.9 8.3 %fusion.30 = bf16[262144]{0:T(1024)(128)(2,1)S(1)} fusion(bf16[4,262144]{1,0:T(4,128)(2,1)S(1)} %all-reduce.2, u32[]{:T(128)} %bitcast.35), kind=kLoop, calls=%fused_computation.46 | loop fusion | bytes 1048580 | tf_op jit(solution)/shard_map/convert.3
  (154 shorter events, 165.1 us)
Async XLA Ops:
  7.2 79.1 %all-gather.4.cloned.1.call-start = ((), (), s32[]{:S(2)}) async-start(), calls=%async_computation.2 | async-start | bytes 4718592 | tf_op jit(solution)/shard_map/all_gather | solution.py:75
  102.0 7.4 copy-start.7
  105.5 41.8 %all-to-all-start = ((bf16[4,2,131072]{2,1,0:T(2,128)(2,1)}), bf16[4,2,131072]{2,1,0:T(2,128)(2,1)S(1)}, u32[]{:S(2)}, u32[]{:S(2)}) async-start(bf16[4,2,131072]{2,1,0:T(2,128)(2,1)} %reshape.398), calls=%async_computation | async-start | bytes 4194304 | tf_op jit(solution)/shard_map/all_to_all | solution.py:82
  112.4 2.9 copy-start.2
  145.7 19.8 %copy-start.5 = (s32[8,32]{0,1:T(8,128)}, s32[8,32]{0,1:T(8,128)S(1)}, u32[]{:S(2)}) copy-start(s32[8,32]{0,1:T(8,128)S(1)} %copy.66) | copy-start | bytes 3076
  145.7 19.7 %copy-start.6 = (s32[8,8,4]{0,2,1:T(4,128)}, s32[8,8,4]{0,2,1:T(4,128)S(1)}, u32[]{:S(2)}) copy-start(s32[8,8,4]{0,2,1:T(4,128)S(1)} %sub.31) | copy-start | bytes 3076
  190.3 2.9 copy-start.3
  197.2 4.6 copy-start
  205.8 12.0 %copy-start.1 = (f32[2048,1536]{0,1:T(8,128)S(1)}, f32[2048,1536]{0,1:T(8,128)}, u32[]{:S(2)}) copy-start(f32[2048,1536]{0,1:T(8,128)} %copy-done) | copy-start | bytes 37748740 | tf_op jit(solution)/shard_map/while
  234.9 4.6 copy-start
  243.5 12.0 %copy-start.1 = (f32[2048,1536]{0,1:T(8,128)S(1)}, f32[2048,1536]{0,1:T(8,128)}, u32[]{:S(2)}) copy-start(f32[2048,1536]{0,1:T(8,128)} %copy-done) | copy-start | bytes 37748740 | tf_op jit(solution)/shard_map/while
  272.5 4.6 copy-start
  281.1 12.0 %copy-start.1 = (f32[2048,1536]{0,1:T(8,128)S(1)}, f32[2048,1536]{0,1:T(8,128)}, u32[]{:S(2)}) copy-start(f32[2048,1536]{0,1:T(8,128)} %copy-done) | copy-start | bytes 37748740 | tf_op jit(solution)/shard_map/while
  310.1 4.6 copy-start
  318.7 12.0 %copy-start.1 = (f32[2048,1536]{0,1:T(8,128)S(1)}, f32[2048,1536]{0,1:T(8,128)}, u32[]{:S(2)}) copy-start(f32[2048,1536]{0,1:T(8,128)} %copy-done) | copy-start | bytes 37748740 | tf_op jit(solution)/shard_map/while
  347.7 4.6 copy-start
  356.3 12.0 %copy-start.1 = (f32[2048,1536]{0,1:T(8,128)S(1)}, f32[2048,1536]{0,1:T(8,128)}, u32[]{:S(2)}) copy-start(f32[2048,1536]{0,1:T(8,128)} %copy-done) | copy-start | bytes 37748740 | tf_op jit(solution)/shard_map/while
  385.3 4.6 copy-start
  393.9 12.0 %copy-start.1 = (f32[2048,1536]{0,1:T(8,128)S(1)}, f32[2048,1536]{0,1:T(8,128)}, u32[]{:S(2)}) copy-start(f32[2048,1536]{0,1:T(8,128)} %copy-done) | copy-start | bytes 37748740 | tf_op jit(solution)/shard_map/while
  419.5 7.1 copy-start.4
  438.2 22.1 %copy-start.8 = (s32[9]{0:T(128)S(1)}, s32[9]{0:T(128)}, u32[]{:S(2)}) copy-start(s32[9]{0:T(128)} %multiply_add_fusion) | copy-start | bytes 112
  483.9 5.1 copy-start.9
  483.9 184.5 %all-to-all-start.1 = ((bf16[8,2,262144]{2,1,0:T(2,128)(2,1)}), bf16[8,2,262144]{2,1,0:T(2,128)(2,1)}, u32[]{:S(2)}, u32[]{:S(2)}) async-start(bf16[8,2,262144]{2,1,0:T(2,128)(2,1)} %reshape.360), calls=%async_computation.1 | async-start | bytes 16777216 | tf_op jit(solution)/shard_map/all_to_all | solution.py:158
Sparse Core Ops, SparseCore 0:
  10.7 75.5 all-gather.3
where the time goes:
time: 780 us; the launch traced here: 771 us
  waiting for transfers between devices  237 us (30%)
  matrix products  187 us (24%)
  local copies, waits for them, and re-layouts  122 us (16%)
  blocking collectives  108 us (14%)
  other arithmetic  92.4 us (12%)
  between operations  14.6 us (2%)
  starting transfers between devices  9.03 us (1%)
    all_to_all x1, waiting for transfers between devices, local(): lax.all_to_all(partials.reshape(n_row, cap_row, flat_width), 'row', split...  170 us
    unnamed x1, blocking collectives  76 us
    dot_general x6, matrix products, pair_grads(): lax.dot_general(gradient_rows, block_value_rows, forward, preferred_eleme...  72.1 us
    all_gather x1, waiting for transfers between devices, local(): lax.all_gather(local_kv, 'row', axis=0, tiled=True)  66.9 us
    convert_element_type x6, other arithmetic, pair_grads(): (weights * (grad_weights - row_delta) * factor).astype(jnp.bfloat16)  40 us
    all_gather x1, blocking collectives, local(): col_lists = lax.all_gather(tile_block_table, 'row', axis=0, tiled=True)  26.1 us
    dot_general x6, matrix products, pair_grads(): lax.dot_general(weights.astype(jnp.bfloat16), gradient_rows, backward, pr...  24.1 us
    dot_general x6, matrix products, pair_grads(): lax.dot_general(grad_scores, tile_query_rows, backward, preferred_element...  22.7 us
  transfers between devices with their start and end apart: 3, of which 2 were waited for; matrix products, arithmetic and copies ran while one was open for 3% of the time, Pallas kernels for 0%

commit v1 on v0

--- a/solution.py
+++ b/solution.py
@@ -72,7 +72,30 @@
     by_col = jnp.transpose(layout, (0, 2, 1, 3)).reshape(n_col, n_col, band_rows)
     col_rank = jnp.cumsum(by_col, axis=2) - by_col
     local_kv = jnp.concatenate((keys, values), axis=1)
-    column = lax.all_gather(local_kv, "row", axis=0, tiled=True).reshape(band_rows, flat_width)
+
+    def view_units(buf):
+        part_now, step_out, item_now = (
+            jax.lax.axis_size("row"),
+            jax.lax.axis_index("row"),
+            buf.shape[0],
+        )
+        frame_out, inter = (buf, 1)
+        while inter < part_now:
+            frame_out = jnp.concatenate(
+                [
+                    frame_out,
+                    jax.lax.ppermute(
+                        frame_out,
+                        axis_name="row",
+                        perm=tuple(((i, (i - inter) % part_now) for i in range(part_now))),
+                    ),
+                ],
+                0,
+            )
+            inter = 2 * inter
+        return jnp.roll(frame_out, step_out * item_now, 0)
+
+    column = view_units(local_kv).reshape(band_rows, flat_width)
     row_wants = by_col[:, my_col, :]
     row_ranks = col_rank[:, my_col, :]
     slot_ids = jnp.arange(blk_dev, dtype=jnp.int32)

time: 780 us -> 838 us (1.074)
  waiting for transfers between devices: 237 us -> 285 us
  local copies, waits for them, and re-layouts: 122 us -> 138 us
  between operations: 14.6 us -> 1.21 us
    ppermute x0 -> x3, waiting for transfers between devices: none -> 114 us  [view_units(): jax.lax.ppermute(frame_out, axis_name='row', perm=tuple(((i, (i - inter)...]
    all_gather x1 -> x0, waiting for transfers between devices: 66.9 us -> none  [local(): lax.all_gather(local_kv, 'row', axis=0, tiled=True)]
    unnamed x26 -> x42, local copies, waits for them, and re-layouts: 13.2 us -> 22.9 us
  transfers between devices with their start and end apart: 3 -> 5, of which waited for: 2 -> 4; matrix products, arithmetic and copies ran while one was open for 3% -> 3% of each run, Pallas kernels for 0% -> 0%
where the time goes in v1:
time: 838 us; the launch traced here: 828 us
  waiting for transfers between devices  285 us (34%)
  matrix products  187 us (22%)
  local copies, waits for them, and re-layouts  138 us (16%)
  blocking collectives  108 us (13%)
  other arithmetic  91.4 us (11%)
  starting transfers between devices  17.3 us (2%)
    all_to_all x1, waiting for transfers between devices, local(): lax.all_to_all(partials.reshape(n_row, cap_row, flat_width), 'row', split...  170 us
    ppermute x3, waiting for transfers between devices, view_units(): jax.lax.ppermute(frame_out, axis_name='row', perm=tuple(((i, (i - inter)...  114 us
    unnamed x1, blocking collectives  76 us
    dot_general x6, matrix products, pair_grads(): lax.dot_general(gradient_rows, block_value_rows, forward, preferred_eleme...  72.1 us
    convert_element_type x6, other arithmetic, pair_grads(): (weights * (grad_weights - row_delta) * factor).astype(jnp.bfloat16)  40 us
    all_gather x1, blocking collectives, local(): col_lists = lax.all_gather(tile_block_table, 'row', axis=0, tiled=True)  26.6 us
    dot_general x6, matrix products, pair_grads(): lax.dot_general(weights.astype(jnp.bfloat16), gradient_rows, backward, pr...  24.1 us
    unnamed x42, local copies, waits for them, and re-layouts  22.9 us
  transfers between devices with their start and end apart: 5, of which 4 were waited for; matrix products, arithmetic and copies ran while one was open for 3% of the time, Pallas kernels for 0%

profile of v1, /device:TPU:0, one launch (start us, length us, event | category | flops | bytes accessed | tf_op | source)
XLA Modules:
  0.0 828.4 jit_solution(13159179320332587707)
XLA Ops:
  4.1 6.0 collective-permute-start
  10.1 11.2 %collective-permute-done = bf16[512,512]{1,0:T(8,128)(2,1)S(1)} collective-permute-done((bf16[512,512]{1,0:T(8,128)(2,1)S(1)}, bf16[512,512]{1,0:T(8,128)(2,1)S(1)}, u32[]{:S(2)}, u32[]{:S(2)}) %collective-permute-start) | collective-permute-done | bytes 524320 | tf_op jit(solution)/shard_map/ppermute | solution.py:87
  29.4 16.0 %collective-permute-done.1 = bf16[1024,512]{1,0:T(8,128)(2,1)S(1)} collective-permute-done((bf16[1024,512]{1,0:T(8,128)(2,1)S(1)}, bf16[1024,512]{1,0:T(8,128)(2,1)S(1)}, u32[]{:S(2)}, u32[]{:S(2)}) %collective-permute-start.1) | collective-permute-done | bytes 1048608 | tf_op jit(solution)/shard_map/ppermute | solution.py:87
  51.8 86.8 %collective-permute-done.2 = bf16[2048,512]{1,0:T(8,128)(2,1)S(1)} collective-permute-done((bf16[2048,512]{1,0:T(8,128)(2,1)}, bf16[2048,512]{1,0:T(8,128)(2,1)S(1)}, u32[]{:S(2)}, u32[]{:S(2)}) %collective-permute-start.2) | collective-permute-done | bytes 2097184 | tf_op jit(solution)/shard_map/ppermute | solution.py:87
  149.4 6.0 reshape.352
  182.6 26.6 %all-gather.1 = s32[8,3,3]{2,1,0:T(4,128)S(1)} all-gather(s32[1,3,3]{2,1,0:T(4,128)S(1)} %bitcast.153), channel_id=1, replica_groups=mesh['row'=8,'col'=4] {'row'}, dimensions={0}, use_global_device_ids=true | all-gather | bytes 324 | tf_op jit(solution)/shard_map/all_gather | solution.py:166
  214.5 14.8 %reduce.2 = bf16[4,262144]{1,0:T(4,128)(2,1)} reduce(bf16[4,1,262144]{2,1,0:T(2,128)(2,1)} %reshape.399, bf16[]{:T(256)} %constant.201), dimensions={1}, to_apply=%all_to_all.6.reduce_sub_computation | reduce | bytes 4194306 | tf_op jit(solution)/shard_map/all_to_all | solution.py:105
  234.9 7.8 gather.20
  242.7 11.5 %fusion.29 = bf16[3,2,2,1536,128]{4,1,2,3,0:T(2,128)(2,1)S(1)} fusion(bf16[3,1536,2,2,128]{4,3,2,1,0:T(2,128)(2,1)} %gather.20, pred[3,1536]{1,0:T(4,128)(4,1)S(1)} %bitcast.154), kind=kLoop, calls=%fused_computation.42 | loop fusion | flops 2359296 | bytes 9441792 | tf_op jit(solution)/shard_map/transpose | solution.py:130
  257.1 226.0 %while.14 = (s32[]{:T(128)}, bf16[6,2048,128]{2,1,0:T(8,128)(2,1)S(1)}, f32[6,1536,128]{2,1,0:T(8,128)}, f32[6,1536,128]{2,1,0:T(8,128)}, s32[6,1536]{1,0:T(8,12...) while((s32[]{:T(128)}, ...), condition=%wide.region_6.7_spmd, body=%wide.region_2.6_spmd.sunk | while | flops 4086294528 | bytes 213654736 | solution.py:150
  269.3 12.0 %multiply_reduce_fusion.2 = (f32[2048]{0:T(1024)S(1)}, f32[2048,1536]{0,1:T(8,128)}) fusion(f32[2048]{0:T(1024)S(1)} %fusion.73, f32[2048,1536]{0,1:T(8,128)} %copy-done, f32[2048]{0:T(1024)S(1)} %get-tuple-element.146, bf16[6,2,1536,128]{3,2,1,0:T(8,128)(2,1)} %get-tuple-element.180, s32[]{:T(128)} %get-tuple-element.161, s32[]{:T(128)S(6)} %add.297, ...), kind=kOutput, calls=%fused_computation.4.clone.1 | convolution fusion | flops 817887232 | bytes 26108932 | tf_op jit(solution)/shard_map/while/body/eval_jaxpr/dot_general | solution.py:29
  281.4 6.7 multiply_convert_fusion.2
  307.0 12.0 %multiply_reduce_fusion.2 = (f32[2048]{0:T(1024)S(1)}, f32[2048,1536]{0,1:T(8,128)}) fusion(f32[2048]{0:T(1024)S(1)} %fusion.73, f32[2048,1536]{0,1:T(8,128)} %copy-done, f32[2048]{0:T(1024)S(1)} %get-tuple-element.146, bf16[6,2,1536,128]{3,2,1,0:T(8,128)(2,1)} %get-tuple-element.180, s32[]{:T(128)} %get-tuple-element.161, s32[]{:T(128)S(6)} %add.297, ...), kind=kOutput, calls=%fused_computation.4.clone.1 | convolution fusion | flops 817887232 | bytes 26108932 | tf_op jit(solution)/shard_map/while/body/eval_jaxpr/dot_general | solution.py:29
  319.0 6.7 multiply_convert_fusion.2
  344.6 12.0 %multiply_reduce_fusion.2 = (f32[2048]{0:T(1024)S(1)}, f32[2048,1536]{0,1:T(8,128)}) fusion(f32[2048]{0:T(1024)S(1)} %fusion.73, f32[2048,1536]{0,1:T(8,128)} %copy-done, f32[2048]{0:T(1024)S(1)} %get-tuple-element.146, bf16[6,2,1536,128]{3,2,1,0:T(8,128)(2,1)} %get-tuple-element.180, s32[]{:T(128)} %get-tuple-element.161, s32[]{:T(128)S(6)} %add.297, ...), kind=kOutput, calls=%fused_computation.4.clone.1 | convolution fusion | flops 817887232 | bytes 26108932 | tf_op jit(solution)/shard_map/while/body/eval_jaxpr/dot_general | solution.py:29
  356.6 6.7 multiply_convert_fusion.2
  382.2 12.0 %multiply_reduce_fusion.2 = (f32[2048]{0:T(1024)S(1)}, f32[2048,1536]{0,1:T(8,128)}) fusion(f32[2048]{0:T(1024)S(1)} %fusion.73, f32[2048,1536]{0,1:T(8,128)} %copy-done, f32[2048]{0:T(1024)S(1)} %get-tuple-element.146, bf16[6,2,1536,128]{3,2,1,0:T(8,128)(2,1)} %get-tuple-element.180, s32[]{:T(128)} %get-tuple-element.161, s32[]{:T(128)S(6)} %add.297, ...), kind=kOutput, calls=%fused_computation.4.clone.1 | convolution fusion | flops 817887232 | bytes 26108932 | tf_op jit(solution)/shard_map/while/body/eval_jaxpr/dot_general | solution.py:29
  394.2 6.7 multiply_convert_fusion.2
  419.8 12.0 %multiply_reduce_fusion.2 = (f32[2048]{0:T(1024)S(1)}, f32[2048,1536]{0,1:T(8,128)}) fusion(f32[2048]{0:T(1024)S(1)} %fusion.73, f32[2048,1536]{0,1:T(8,128)} %copy-done, f32[2048]{0:T(1024)S(1)} %get-tuple-element.146, bf16[6,2,1536,128]{3,2,1,0:T(8,128)(2,1)} %get-tuple-element.180, s32[]{:T(128)} %get-tuple-element.161, s32[]{:T(128)S(6)} %add.297, ...), kind=kOutput, calls=%fused_computation.4.clone.1 | convolution fusion | flops 817887232 | bytes 26108932 | tf_op jit(solution)/shard_map/while/body/eval_jaxpr/dot_general | solution.py:29
  431.8 6.7 multiply_convert_fusion.2
  457.4 12.0 %multiply_reduce_fusion.2 = (f32[2048]{0:T(1024)S(1)}, f32[2048,1536]{0,1:T(8,128)}) fusion(f32[2048]{0:T(1024)S(1)} %fusion.73, f32[2048,1536]{0,1:T(8,128)} %copy-done, f32[2048]{0:T(1024)S(1)} %get-tuple-element.146, bf16[6,2,1536,128]{3,2,1,0:T(8,128)(2,1)} %get-tuple-element.180, s32[]{:T(128)} %get-tuple-element.161, s32[]{:T(128)S(6)} %add.297, ...), kind=kOutput, calls=%fused_computation.4.clone.1 | convolution fusion | flops 817887232 | bytes 26108932 | tf_op jit(solution)/shard_map/while/body/eval_jaxpr/dot_general | solution.py:29
  469.4 6.7 multiply_convert_fusion.2
  483.1 7.1 copy.68
  490.2 6.0 copy.69
  496.2 5.5 maximum_bitcast_fusion
  501.7 22.3 %reshape.359 = f32[9,262144]{1,0:T(8,128)} reshape(f32[3,3,512,2,2,128]{5,4,3,2,1,0:T(2,128)} %maximum_bitcast_fusion) | data formatting | bytes 18874368 | tf_op jit(solution)/shard_map/reshape | solution.py:162
  524.1 13.9 %convolution_convert_fusion = bf16[16,262144]{1,0:T(8,128)(2,1)} fusion(f32[9,262144]{1,0:T(8,128)} %reshape.359, s32[9]{0:T(128)S(1)} %copy-done.12), kind=kOutput, calls=%fused_computation.35 | convolution fusion | flops 457179264 | bytes 17825828 | tf_op jit(solution)/shard_map/dot_general | solution.py:178
  538.0 9.5 %reshape.360 = bf16[8,2,262144]{2,1,0:T(2,128)(2,1)} reshape(bf16[16,262144]{1,0:T(8,128)(2,1)} %convolution_convert_fusion) | data formatting | bytes 16777216 | tf_op jit(solution)/shard_map/reshape | solution.py:182
  561.7 170.5 %all-to-all-done.1 = bf16[8,2,262144]{2,1,0:T(2,128)(2,1)} async-done(((bf16[8,2,262144]{2,1,0:T(2,128)(2,1)}), bf16[8,2,262144]{2,1,0:T(2,128)(2,1)}, u32[]{:S(2)}, u32[]{:S(2)}) %all-to-all-start.1) | async-done | bytes 8388640 | tf_op jit(solution)/shard_map/all_to_all | solution.py:181
  732.2 10.5 %convolution_bitcast_fusion.2 = f32[4,262144]{1,0:T(4,128)} fusion(bf16[8,2,262144]{2,1,0:T(2,128)(2,1)} %all-to-all-done.1, s32[8,4]{0,1:T(4,128)S(1)} %dynamic-slice_bitcast_fusion.5, pred[8,4]{0,1:T(4,128)(4,1)S(1)} %fusion.43), kind=kOutput, calls=%fused_computation.36 | convolution fusion | flops 33554560 | bytes 12583072 | tf_op jit(solution)/shard_map/dot_general | solution.py:193
  742.7 76.0 %all-reduce.2 = bf16[4,262144]{1,0:T(4,128)(2,1)S(1)} all-reduce(f32[4,262144]{1,0:T(4,128)} %convolution_bitcast_fusion.2), channel_id=2, replica_groups=mesh['row'=8,'col'=4] {'col'}, use_global_device_ids=true, to_apply=%region_9.10.clone | all-reduce | flops 1048576 | bytes 6291456
  818.7 8.3 fusion.30
  (177 shorter events, 198.1 us)
Async XLA Ops:
  0.6 46.8 %copy-start.11 = (s32[3,3]{1,0:T(4,128)S(1)}, s32[3,3]{1,0:T(4,128)}, u32[]{:S(2)}) copy-start(s32[3,3]{1,0:T(4,128)} %param.11) | copy-start | bytes 112
  4.1 17.2 %collective-permute-start = (bf16[512,512]{1,0:T(8,128)(2,1)S(1)}, bf16[512,512]{1,0:T(8,128)(2,1)S(1)}, u32[]{:S(2)}, u32[]{:S(2)}) collective-permute-start(bf16[512,512]{1,0:T(8,128)(2,1)S(1)} %get-tuple-element.82), channel_id=1, source_target_pairs={{0,28},{4,0},{8,4},{12,8},{16,12},{20,16},{24,20},{28,24},{1,29},{... | collective-permute-start | bytes 1572872 | tf_op jit(solution)/shard_map/ppermute | solution.py:87
  21.3 24.2 %copy-start.2 = (bf16[512,512]{1,0:T(8,128)(2,1)}, bf16[512,512]{1,0:T(8,128)(2,1)S(1)}, u32[]{:S(2)}) copy-start(bf16[512,512]{1,0:T(8,128)(2,1)S(1)} %collective-permute-done) | copy-start | bytes 1572868
  21.4 118.7 %copy-start.7 = (bf16[512,256]{1,0:T(8,128)(2,1)S(1)}, bf16[512,256]{1,0:T(8,128)(2,1)}, u32[]{:S(2)}) copy-start(bf16[512,256]{1,0:T(8,128)(2,1)} %param.8) | copy-start | bytes 786436
  21.4 24.1 %collective-permute-start.1 = (bf16[1024,512]{1,0:T(8,128)(2,1)S(1)}, bf16[1024,512]{1,0:T(8,128)(2,1)S(1)}, u32[]{:S(2)}, u32[]{:S(2)}) collective-permute-start(bf16[1024,512]{1,0:T(8,128)(2,1)S(1)} %pad_maximum_fusion.1), channel_id=1, source_target_pairs={{0,24},{4,28},{8,0},{12,4},{16,8},{20,12},{24,16},{28,20},{1,25},{... | collective-permute-start | bytes 3145736 | tf_op jit(solution)/shard_map/ppermute | solution.py:87
  46.9 91.7 %collective-permute-start.2 = (bf16[2048,512]{1,0:T(8,128)(2,1)}, bf16[2048,512]{1,0:T(8,128)(2,1)S(1)}, u32[]{:S(2)}, u32[]{:S(2)}) collective-permute-start(bf16[2048,512]{1,0:T(8,128)(2,1)} %pad_maximum_fusion), channel_id=1, source_target_pairs={{0,16},{4,20},{8,24},{12,28},{16,0},{20,4},{24,8},{28,12},{1,17},{... | collective-permute-start | bytes 6291464 | tf_op jit(solution)/shard_map/ppermute | solution.py:87
  48.4 92.4 %copy-start.8 = (bf16[512,256]{1,0:T(8,128)(2,1)S(1)}, bf16[512,256]{1,0:T(8,128)(2,1)}, u32[]{:S(2)}) copy-start(bf16[512,256]{1,0:T(8,128)(2,1)} %param.9) | copy-start | bytes 786436
  48.4 93.2 %copy-start.3 = (bf16[512,512]{1,0:T(8,128)(2,1)S(1)}, bf16[512,512]{1,0:T(8,128)(2,1)}, u32[]{:S(2)}) copy-start(bf16[512,512]{1,0:T(8,128)(2,1)} %copy-done.2) | copy-start | bytes 1572868
  168.6 42.5 %all-to-all-start = ((bf16[4,2,131072]{2,1,0:T(2,128)(2,1)}), bf16[4,2,131072]{2,1,0:T(2,128)(2,1)S(1)}, u32[]{:S(2)}, u32[]{:S(2)}) async-start(bf16[4,2,131072]{2,1,0:T(2,128)(2,1)} %reshape.398), calls=%async_computation | async-start | bytes 4194304 | tf_op jit(solution)/shard_map/all_to_all | solution.py:105
  172.9 5.8 copy-start.4
  209.5 19.8 %copy-start.9 = (s32[8,32]{0,1:T(8,128)}, s32[8,32]{0,1:T(8,128)S(1)}, u32[]{:S(2)}) copy-start(s32[8,32]{0,1:T(8,128)S(1)} %copy.66) | copy-start | bytes 3076
  209.6 19.7 %copy-start.10 = (s32[8,8,4]{0,2,1:T(4,128)}, s32[8,8,4]{0,2,1:T(4,128)S(1)}, u32[]{:S(2)}) copy-start(s32[8,8,4]{0,2,1:T(4,128)S(1)} %sub.36) | copy-start | bytes 3076
  254.2 2.9 copy-start.5
  260.8 4.6 copy-start
  269.3 12.0 %copy-start.1 = (f32[2048,1536]{0,1:T(8,128)S(1)}, f32[2048,1536]{0,1:T(8,128)}, u32[]{:S(2)}) copy-start(f32[2048,1536]{0,1:T(8,128)} %copy-done) | copy-start | bytes 37748740 | tf_op jit(solution)/shard_map/while
  298.4 4.6 copy-start
  307.0 12.0 %copy-start.1 = (f32[2048,1536]{0,1:T(8,128)S(1)}, f32[2048,1536]{0,1:T(8,128)}, u32[]{:S(2)}) copy-start(f32[2048,1536]{0,1:T(8,128)} %copy-done) | copy-start | bytes 37748740 | tf_op jit(solution)/shard_map/while
  336.0 4.6 copy-start
  344.6 12.0 %copy-start.1 = (f32[2048,1536]{0,1:T(8,128)S(1)}, f32[2048,1536]{0,1:T(8,128)}, u32[]{:S(2)}) copy-start(f32[2048,1536]{0,1:T(8,128)} %copy-done) | copy-start | bytes 37748740 | tf_op jit(solution)/shard_map/while
  373.6 4.6 copy-start
  382.2 12.0 %copy-start.1 = (f32[2048,1536]{0,1:T(8,128)S(1)}, f32[2048,1536]{0,1:T(8,128)}, u32[]{:S(2)}) copy-start(f32[2048,1536]{0,1:T(8,128)} %copy-done) | copy-start | bytes 37748740 | tf_op jit(solution)/shard_map/while
  411.2 4.6 copy-start
  419.8 12.0 %copy-start.1 = (f32[2048,1536]{0,1:T(8,128)S(1)}, f32[2048,1536]{0,1:T(8,128)}, u32[]{:S(2)}) copy-start(f32[2048,1536]{0,1:T(8,128)} %copy-done) | copy-start | bytes 37748740 | tf_op jit(solution)/shard_map/while
  448.8 4.6 copy-start
  457.4 12.0 %copy-start.1 = (f32[2048,1536]{0,1:T(8,128)S(1)}, f32[2048,1536]{0,1:T(8,128)}, u32[]{:S(2)}) copy-start(f32[2048,1536]{0,1:T(8,128)} %copy-done) | copy-start | bytes 37748740 | tf_op jit(solution)/shard_map/while
  483.1 13.1 %copy-start.6 = (bf16[6,2048,128]{2,1,0:T(8,128)(2,1)}, bf16[6,2048,128]{2,1,0:T(8,128)(2,1)S(1)}, u32[]{:S(2)}) copy-start(bf16[6,2048,128]{2,1,0:T(8,128)(2,1)S(1)} %get-tuple-element.52) | copy-start | bytes 9437188
  501.7 22.3 %copy-start.12 = (s32[9]{0:T(128)S(1)}, s32[9]{0:T(128)}, u32[]{:S(2)}) copy-start(s32[9]{0:T(128)} %multiply_add_fusion) | copy-start | bytes 112
  547.4 5.1 copy-start.13
  547.4 184.8 %all-to-all-start.1 = ((bf16[8,2,262144]{2,1,0:T(2,128)(2,1)}), bf16[8,2,262144]{2,1,0:T(2,128)(2,1)}, u32[]{:S(2)}, u32[]{:S(2)}) async-start(bf16[8,2,262144]{2,1,0:T(2,128)(2,1)} %reshape.360), calls=%async_computation.1 | async-start | bytes 16777216 | tf_op jit(solution)/shard_map/all_to_all | solution.py:181
